TPU v7x, 32 devices: a whole 2x2x4 slice. The times are simulated.
32 devices in a mesh: groups: 2 (over x), row: 4 (over y, core), col: 4 (over z).
Axes of the slice: x: 2, y: 2, z: 4, core: 2. Of those that a mesh axis runs over, the one named last changes fastest.
Arguments:
- observed: float32 [2048, 2048], P(('groups', 'row'), 'col'), parts along dimension 0, may hold values from -24 to 24
- estimate: float32 [2048, 2048], P(('groups', 'row'), 'col'), parts along dimension 0, may hold values from -6 to 6
- kernel: float32 [512, 256], P(('groups', 'row')), parts along dimension 0, may hold values from -6 to 6
Outputs:
- refined: float32 [2048, 2048], P(('groups', 'row'), 'col'), parts along dimension 0
- new_kernel: float32 [512, 256], P(('groups', 'row')), parts along dimension 0
There are 2 independent parts, one for each index of `groups`. A program takes and returns all parts, laid end to end along the dimension named above; each array names one. Nothing has to cross between parts.
All inputs are finite; a program needn't handle non-finite values.
Results may differ from a plain program's by a relative error of at most 0.0001.
Values sent between devices are 32-bit elements; how exact they have to be, the bound alone decides.
A program may use at most 128 MiB of HBM per device.

v0:
```python
import math

import jax
import jax.numpy as jnp
from jax import lax
from jax.sharding import PartitionSpec as P

HIGHEST = lax.Precision.HIGHEST
EPSILON = 1e-06


def padded(block, sides, width):
    for axis, dim in sides:
        count = lax.axis_size(axis)
        forward = [(i, i + 1) for i in range(count - 1)]
        backward = [(target, source) for source, target in forward]
        low = lax.ppermute(
            lax.slice_in_dim(block, block.shape[dim] - width, None, axis=dim), axis, forward
        )
        high = lax.ppermute(lax.slice_in_dim(block, 0, width, axis=dim), axis, backward)
        block = jnp.concatenate([low, block, high], axis=dim)
    return block


def tables(places, length):
    freqs = jnp.arange(length, dtype=jnp.int32)
    phase = jnp.mod(places[:, None] * freqs[None, :], length).astype(jnp.float32) * (
        2.0 * math.pi / length
    )
    return (jnp.cos(phase), jnp.sin(phase))


def forward(field, row_tables, col_tables):
    rows_long = row_tables[0].shape[1]
    cols_long = col_tables[0].shape[1]
    across = jnp.dot(field, jnp.concatenate(col_tables, 1), precision=HIGHEST)
    stacked = lax.dot_general(
        jnp.concatenate(row_tables, 1), across, (((0,), (0,)), ((), ())), precision=HIGHEST
    )
    real_part = stacked[:rows_long, :cols_long] - stacked[rows_long:, cols_long:]
    imag_part = -(stacked[rows_long:, :cols_long] + stacked[:rows_long, cols_long:])
    return (real_part, imag_part)


def inverse(real_part, imag_part, row_tables, col_tables):
    rows_long, cols_long = real_part.shape
    out_rows = row_tables[0].shape[0]
    stacked = jnp.dot(
        jnp.concatenate(row_tables, 0),
        jnp.concatenate([real_part, imag_part], 1),
        precision=HIGHEST,
    )
    mixed_re = stacked[:out_rows, :cols_long] - stacked[out_rows:, cols_long:]
    mixed_im = stacked[out_rows:, :cols_long] + stacked[:out_rows, cols_long:]
    result = lax.dot_general(
        jnp.concatenate([mixed_re, mixed_im], 1),
        jnp.concatenate([col_tables[0], -col_tables[1]], 1),
        (((1,), (1,)), ((), ())),
        precision=HIGHEST,
    )
    return result / (rows_long * cols_long)


def collect(kernel):
    return lax.all_gather(kernel, "row", axis=0, tiled=True)


def per_device(observed, estimate, kernel):
    tile_rows, tile_cols = observed.shape
    owner_rows, kernel_side = kernel.shape
    margin = kernel_side // 2
    rows_long = tile_rows + kernel_side
    cols_long = tile_cols + kernel_side
    factor = 1.0 / kernel_side
    ext_rows = tables(jnp.arange(rows_long, dtype=jnp.int32), rows_long)
    ext_cols = tables(jnp.arange(cols_long, dtype=jnp.int32), cols_long)
    own_rows = tables(jnp.arange(tile_rows, dtype=jnp.int32) + margin, rows_long)
    own_cols = tables(jnp.arange(tile_cols, dtype=jnp.int32) + margin, cols_long)
    lag_rows = tables(jnp.arange(kernel_side, dtype=jnp.int32) - margin, rows_long)
    lag_cols = tables(jnp.arange(kernel_side, dtype=jnp.int32) - margin, cols_long)
    image = estimate
    owned = kernel
    full_kernel = collect(kernel)
    widened = padded(image, (("row", 0), ("col", 1)), margin)
    image_re, image_im = forward(widened, ext_rows, ext_cols)
    kernel_re, kernel_im = forward(full_kernel, lag_rows, lag_cols)
    predicted = (
        inverse(
            image_re * kernel_re - image_im * kernel_im,
            image_re * kernel_im + image_im * kernel_re,
            own_rows,
            own_cols,
        )
        * factor
    )
    residual = predicted - observed
    local_squares = jnp.sum(residual * residual)
    loss = 0.5 * lax.psum(local_squares, ("row", "col"))
    wide_residual = padded(residual, (("row", 0), ("col", 1)), margin)
    resid_re, resid_im = forward(wide_residual, ext_rows, ext_cols)
    image_grad = (
        inverse(
            resid_re * kernel_re + resid_im * kernel_im,
            resid_im * kernel_re - resid_re * kernel_im,
            own_rows,
            own_cols,
        )
        * factor
    )
    tile_re, tile_im = forward(residual, own_rows, own_cols)
    kernel_grad = (
        inverse(
            tile_re * image_re + tile_im * image_im,
            tile_im * image_re - tile_re * image_im,
            lag_rows,
            lag_cols,
        )
        * factor
    )
    grad_squares = jnp.sum(image_grad * image_grad)
    image_norm = lax.psum(grad_squares, ("row", "col"))
    owner_grad = lax.psum_scatter(kernel_grad, "row", scatter_dimension=0, tiled=True)
    owner_grad = lax.psum(owner_grad, "col")
    kernel_norm = lax.psum(jnp.sum(owner_grad * owner_grad), "row")
    owned = owned - 0.25 * loss / (kernel_norm + EPSILON) * owner_grad
    image = image - loss / (image_norm + EPSILON) * image_grad
    return (image, owned)


def solution(mesh):
    placed = (P(("groups", "row"), "col"), P(("groups", "row"), "col"), P(("groups", "row"), None))
    return jax.shard_map(
        per_device,
        mesh=mesh,
        in_specs=placed,
        out_specs=(P(("groups", "row"), "col"), P(("groups", "row"), None)),
        check_vma=False,
    )
```

profile of v0, /device:TPU:0, one launch (start us, length us, event | category | flops | bytes accessed | tf_op | source)
XLA Modules:
  0.0 264.4 jit_solution(6838239969392656546)
XLA Ops:
  12.0 4.3 %fusion.109 = (f32[256,768]{1,0:T(8,128)}, f32[256,768]{1,0:T(8,128)S(1)}, f32[256,768]{1,0:T(8,128)S(1)}) fusion(s32[256]{0:T(256)S(1)} %iota_add_fusion.1), kind=kLoop, calls=%fused_computation.148 | loop fusion | flops 1966080 | bytes 2360320 | tf_op jit(solution)/shard_map/neg | solution.py:57
  18.4 9.1 %all_gather.3 = f32[256,256]{1,0:T(8,128)S(1)} all-gather(f32[64,256]{1,0:T(8,128)S(1)} %copy-done.28), channel_id=1, replica_groups=mesh['groups'=2,'row'=4,'col'=4] {'row'}, dimensions={0}, use_global_device_ids=true | all-gather | bytes 327680 | tf_op jit(solution)/shard_map/all_gather | solution.py:65
  27.5 8.0 %fusion.58 = (f32[512,768]{1,0:T(8,128)}, f32[512,768]{1,0:T(8,128)}, f32[512,768]{1,0:T(8,128)S(1)}) fusion(s32[512]{0:T(512)S(1)} %iota_add_fusion), kind=kLoop, calls=%fused_computation.80 | loop fusion | flops 3932160 | bytes 4720640 | tf_op jit(solution)/shard_map/sin | solution.py:30
  38.3 11.2 %fusion.64 = f32[1024,1536]{1,0:T(8,128)S(1)} fusion(f32[1536,256]{1,0:T(8,128)S(1)} %fusion.27, f32[256,512]{1,0:T(8,128)S(1)} %get-tuple-element.36, f32[256,512]{1,0:T(8,128)S(1)} %get-tuple-element.35), kind=kOutput, calls=%fused_computation.93 | convolution fusion | flops 4832100352 | bytes 8912896 | tf_op jit(solution)/shard_map/dot_general | solution.py:37
  49.5 9.5 %fusion.22 = (f32[768,768]{1,0:T(8,128)S(1)}, f32[768,768]{1,0:T(8,128)S(1)}) fusion(), kind=kLoop, calls=%fused_computation.28 | loop fusion | flops 5308416 | bytes 4718592 | tf_op jit(solution)/shard_map/sin | solution.py:30
  59.0 4.3 %fusion.103 = (f32[512,512]{1,0:T(8,128)S(1)}, f32[512,512]{1,0:T(8,128)S(1)}) fusion(), kind=kLoop, calls=%fused_computation.142 | loop fusion | flops 3670016 | bytes 2097152 | tf_op jit(solution)/shard_map/sin | solution.py:30
  63.5 3.5 %collective-permute-start.2 = (f32[512,128]{1,0:T(8,128)S(1)}, f32[512,128]{1,0:T(8,128)S(1)}, u32[]{:S(2)}, u32[]{:S(2)}) collective-permute-start(f32[512,128]{1,0:T(8,128)S(1)} %get-tuple-element.21), channel_id=1, source_target_pairs={{0,1},{1,2},{2,3},{4,5},{5,6},{6,7},{8,9},{9,10},{10,11},{12,13},{... | collective-permute-start | bytes 786440 | tf_op jit(solution)/shard_map/ppermute | solution.py:17
  68.3 3.2 %fusion.113 = (f32[256,512]{1,0:T(8,128)}, f32[256,512]{1,0:T(8,128)}) fusion(s32[256]{0:T(256)S(1)} %iota_add_fusion.2), kind=kLoop, calls=%fused_computation.155 | loop fusion | flops 1835008 | bytes 1049600 | tf_op jit(solution)/shard_map/cos | solution.py:30
  73.0 4.1 %collective-permute-done.3 = f32[512,128]{1,0:T(8,128)S(1)} collective-permute-done((f32[512,128]{1,0:T(8,128)S(1)}, f32[512,128]{1,0:T(8,128)S(1)}, u32[]{:S(2)}, u32[]{:S(2)}) %collective-permute-start.3) | collective-permute-done | bytes 262176 | tf_op jit(solution)/shard_map/ppermute | solution.py:20
  77.2 7.7 %fusion.1 = f32[512,1536]{1,0:T(8,128)S(1)} fusion(f32[768,768]{1,0:T(8,128)S(1)} %get-tuple-element.41, f32[768,768]{1,0:T(8,128)S(1)} %get-tuple-element.42, f32[512,128]{1,0:T(8,128)S(1)} %collective-permute-done.3, f32[512,512]{1,0:T(8,128)S(1)} %constant_dynamic-update-slice_fusion, f32[512,128]{1,0:T(8,128)S(1)} %collective-permute-done.2), kind=kOutput, calls=%fused_computation.2 | convolution fusion | flops 7249723392 | bytes 9437184 | tf_op jit(solution)/shard_map/dot_general | solution.py:36
  84.9 11.5 %fusion.26 = f32[1024,1536]{1,0:T(8,128)S(1)} fusion(f32[512,1536]{1,0:T(8,128)S(1)} %fusion.1, f32[512,512]{1,0:T(8,128)S(1)} %get-tuple-element.43, f32[512,512]{1,0:T(8,128)S(1)} %get-tuple-element.44), kind=kOutput, calls=%fused_computation.35 | convolution fusion | flops 9664200704 | bytes 11534336 | tf_op jit(solution)/shard_map/dot_general | solution.py:37
  102.6 5.4 %fusion.3 = f32[512,1536]{1,0:T(8,128)S(1)} fusion(f32[512,768]{1,0:T(8,128)S(1)} %multiply_add_fusion.2, f32[512,768]{1,0:T(8,128)S(1)} %copy-done.16, f32[256,512]{1,0:T(8,128)S(1)} %copy-done.11, f32[256,512]{1,0:T(8,128)S(1)} %copy-done.9), kind=kOutput, calls=%fused_computation.7 | convolution fusion | flops 4832886784 | bytes 7340032 | tf_op jit(solution)/shard_map/dot_general | solution.py:48
  109.5 3.7 %multiply_reduce_fusion.1 = (f32[]{:T(128)}, f32[256,512]{1,0:T(8,128)S(1)}) fusion(f32[256,512]{1,0:T(8,128)S(1)} %copy-done.27, f32[512,768]{1,0:T(8,128)S(1)} %get-tuple-element.29, f32[512,768]{1,0:T(8,128)S(1)} %copy-done.3, f32[256,768]{1,0:T(8,128)S(1)} %get-tuple-element.18, f32[256,768]{1,0:T(8,128)S(1)} %get-tuple-element.17), kind=kOutput, calls=%fused_computation.139 | convolution fusion | flops 2417623040 | bytes 5767172 | tf_op jit(solution)/shard_map/dot_general | solution.py:55
  116.1 5.6 %fusion.71 = f32[1024,1536]{1,0:T(8,128)S(1)} fusion(f32[256,1536]{1,0:T(8,128)S(1)} %fusion.2, f32[256,512]{1,0:T(8,128)S(1)} %copy-done.11, f32[256,512]{1,0:T(8,128)S(1)} %copy-done.9), kind=kOutput, calls=%fused_computation.100 | convolution fusion | flops 4832100352 | bytes 8912896 | tf_op jit(solution)/shard_map/dot_general | solution.py:37
  125.3 5.4 %fusion.12 = f32[512,1536]{1,0:T(8,128)S(1)} fusion(f32[512,768]{1,0:T(8,128)S(1)} %get-tuple-element.10, f32[512,768]{1,0:T(8,128)S(1)} %get-tuple-element.9, f32[256,512]{1,0:T(8,128)S(1)} %copy-done.23, f32[256,512]{1,0:T(8,128)S(1)} %copy-done.21), kind=kOutput, calls=%fused_computation.16 | convolution fusion | flops 4832886784 | bytes 7340032 | tf_op jit(solution)/shard_map/dot_general | solution.py:48
  131.7 4.2 %collective-permute-start.6 = (f32[512,128]{1,0:T(8,128)}, f32[512,128]{1,0:T(8,128)}, u32[]{:S(2)}, u32[]{:S(2)}) collective-permute-start(f32[512,128]{1,0:T(8,128)} %get-tuple-element.19), channel_id=1, source_target_pairs={{0,1},{1,2},{2,3},{4,5},{5,6},{6,7},{8,9},{9,10},{10,11},{12,13},{... | collective-permute-start | bytes 786440 | tf_op jit(solution)/shard_map/ppermute | solution.py:17
  140.2 5.5 %collective-permute-done.7 = f32[512,128]{1,0:T(8,128)} collective-permute-done((f32[512,128]{1,0:T(8,128)}, f32[512,128]{1,0:T(8,128)}, u32[]{:S(2)}, u32[]{:S(2)}) %collective-permute-start.7) | collective-permute-done | bytes 262176 | tf_op jit(solution)/shard_map/ppermute | solution.py:20
  145.7 10.6 %fusion = f32[512,1536]{1,0:T(8,128)S(1)} fusion(f32[768,768]{1,0:T(8,128)} %copy-done.25, f32[768,768]{1,0:T(8,128)} %copy-done.26, f32[512,128]{1,0:T(8,128)} %collective-permute-done.7, f32[128,512]{1,0:T(8,128)} %copy-done.29, f32[256,512]{1,0:T(8,128)} %copy-done.13, f32[128,512]{1,0:T(8,128)S(1)} %collective-permute-done.4, ...), kind=kOutput, calls=%fused_computation.1 | convolution fusion | flops 7250509824 | bytes 9437184 | tf_op jit(solution)/shard_map/dot_general | solution.py:36
  156.3 10.9 %fusion.25 = f32[1024,1536]{1,0:T(8,128)S(1)} fusion(f32[512,1536]{1,0:T(8,128)S(1)} %fusion, f32[512,512]{1,0:T(8,128)S(1)} %copy-done.6, f32[512,512]{1,0:T(8,128)S(1)} %copy-done.8), kind=kOutput, calls=%fused_computation.34 | convolution fusion | flops 9664200704 | bytes 11534336 | tf_op jit(solution)/shard_map/dot_general | solution.py:37
  168.5 5.6 %fusion.7 = f32[512,1536]{1,0:T(8,128)S(1)} fusion(f32[512,768]{1,0:T(8,128)S(1)} %get-tuple-element.12, f32[512,768]{1,0:T(8,128)S(1)} %get-tuple-element.11, f32[256,512]{1,0:T(8,128)S(1)} %copy-done.12, f32[256,512]{1,0:T(8,128)S(1)} %copy-done.10), kind=kOutput, calls=%fused_computation.11 | convolution fusion | flops 4832886784 | bytes 7340032 | tf_op jit(solution)/shard_map/dot_general | solution.py:48
  175.5 3.5 %multiply_reduce_fusion = (f32[]{:T(128)}, f32[256,512]{1,0:T(8,128)S(1)}) fusion(f32[512,768]{1,0:T(8,128)S(1)} %get-tuple-element.29, f32[512,768]{1,0:T(8,128)S(1)} %copy-done.4, f32[256,768]{1,0:T(8,128)S(1)} %get-tuple-element.16, f32[256,768]{1,0:T(8,128)S(1)} %get-tuple-element.15), kind=kOutput, calls=%fused_computation.138 | convolution fusion | flops 2417491968 | bytes 5242884 | tf_op jit(solution)/shard_map/dot_general | solution.py:55
  179.0 31.1 %all-reduce = (f32[]{:T(128)}, f32[]{:T(128)}) all-reduce(f32[]{:T(128)} %get-tuple-element.37, f32[]{:T(128)} %get-tuple-element.39), channel_id=1, replica_groups=mesh['groups'=2,'row'=4,'col'=4] {'row','col'}, use_global_device_ids=true, to_apply=%region_1.2 | all-reduce | flops 2 | bytes 16 | tf_op jit(solution)/shard_map/psum | solution.py:98
  212.4 34.5 %all-reduce.3.cloned.1.call-done = f32[64,256]{1,0:T(8,128)} async-done(((f32[64,256]{1,0:T(8,128)}), f32[64,256]{1,0:T(8,128)}) %all-reduce.3.cloned.1.call-update) | async-done | bytes 65552 | tf_op jit(solution)/shard_map/psum | solution.py:123
  249.0 6.2 %psum.31 = f32[]{:T(128)} all-reduce(f32[]{:T(128)} %multiply_reduce_fusion.2), channel_id=1, replica_groups=mesh['groups'=2,'row'=4,'col'=4] {'row'}, use_global_device_ids=true, to_apply=%region_7.8 | all-reduce | flops 1 | bytes 8 | tf_op jit(solution)/shard_map/psum | solution.py:124
  (101 shorter events, 38.2 us)
Async XLA Ops:
  7.2 204.3 %reduce-scatter.2.cloned.1.call-start = ((), (), s32[]{:S(2)}) async-start(), calls=%async_computation.1 | async-start | bytes 327680 | tf_op jit(solution)/shard_map/reduce_scatter | solution.py:122
  8.3 55.1 %collective-permute-start = (f32[128,512]{1,0:T(8,128)S(1)}, f32[128,512]{1,0:T(8,128)S(1)}, u32[]{:S(2)}, u32[]{:S(2)}) collective-permute-start(f32[128,512]{1,0:T(8,128)S(1)} %get-tuple-element.26), channel_id=1, source_target_pairs={{0,4},{4,8},{8,12},{1,5},{5,9},{9,13},{2,6},{6,10},{10,14},{3,7},{... | collective-permute-start | bytes 786440 | tf_op jit(solution)/shard_map/ppermute | solution.py:17
  10.7 52.8 %collective-permute-start.1 = (f32[128,512]{1,0:T(8,128)S(1)}, f32[128,512]{1,0:T(8,128)S(1)}, u32[]{:S(2)}, u32[]{:S(2)}) collective-permute-start(f32[128,512]{1,0:T(8,128)S(1)} %get-tuple-element.25), channel_id=1, source_target_pairs={{4,0},{8,4},{12,8},{5,1},{9,5},{13,9},{6,2},{10,6},{14,10},{7,3},{... | collective-permute-start | bytes 786440 | tf_op jit(solution)/shard_map/ppermute | solution.py:20
  16.2 19.3 %copy-start.14 = (f32[256,768]{1,0:T(8,128)}, f32[256,768]{1,0:T(8,128)S(1)}, u32[]{:S(2)}) copy-start(f32[256,768]{1,0:T(8,128)S(1)} %get-tuple-element.32) | copy-start | bytes 2359300
  18.4 19.9 %copy-start.20 = (f32[256,512]{1,0:T(8,128)}, f32[256,512]{1,0:T(8,128)S(1)}, u32[]{:S(2)}) copy-start(f32[256,512]{1,0:T(8,128)S(1)} %get-tuple-element.35) | copy-start | bytes 1572868
  18.4 19.9 %copy-start.22 = (f32[256,512]{1,0:T(8,128)}, f32[256,512]{1,0:T(8,128)S(1)}, u32[]{:S(2)}) copy-start(f32[256,512]{1,0:T(8,128)S(1)} %get-tuple-element.36) | copy-start | bytes 1572868
  59.0 18.2 %copy-start.25 = (f32[768,768]{1,0:T(8,128)}, f32[768,768]{1,0:T(8,128)S(1)}, u32[]{:S(2)}) copy-start(f32[768,768]{1,0:T(8,128)S(1)} %get-tuple-element.41) | copy-start | bytes 7077892
  59.0 18.2 %copy-start.26 = (f32[768,768]{1,0:T(8,128)}, f32[768,768]{1,0:T(8,128)S(1)}, u32[]{:S(2)}) copy-start(f32[768,768]{1,0:T(8,128)S(1)} %get-tuple-element.42) | copy-start | bytes 7077892
  63.3 21.6 %copy-start.5 = (f32[512,512]{1,0:T(8,128)}, f32[512,512]{1,0:T(8,128)S(1)}, u32[]{:S(2)}) copy-start(f32[512,512]{1,0:T(8,128)S(1)} %get-tuple-element.43) | copy-start | bytes 3145732
  63.3 21.6 %copy-start.7 = (f32[512,512]{1,0:T(8,128)}, f32[512,512]{1,0:T(8,128)S(1)}, u32[]{:S(2)}) copy-start(f32[512,512]{1,0:T(8,128)S(1)} %get-tuple-element.44) | copy-start | bytes 3145732
  63.5 9.5 %collective-permute-start.2 = (f32[512,128]{1,0:T(8,128)S(1)}, f32[512,128]{1,0:T(8,128)S(1)}, u32[]{:S(2)}, u32[]{:S(2)}) collective-permute-start(f32[512,128]{1,0:T(8,128)S(1)} %get-tuple-element.21), channel_id=1, source_target_pairs={{0,1},{1,2},{2,3},{4,5},{5,6},{6,7},{8,9},{9,10},{10,11},{12,13},{... | collective-permute-start | bytes 786440 | tf_op jit(solution)/shard_map/ppermute | solution.py:17
  67.0 10.2 %collective-permute-start.3 = (f32[512,128]{1,0:T(8,128)S(1)}, f32[512,128]{1,0:T(8,128)S(1)}, u32[]{:S(2)}, u32[]{:S(2)}) collective-permute-start(f32[512,128]{1,0:T(8,128)S(1)} %get-tuple-element.22), channel_id=1, source_target_pairs={{1,0},{2,1},{3,2},{5,4},{6,5},{7,6},{9,8},{10,9},{11,10},{13,12},{... | collective-permute-start | bytes 786440 | tf_op jit(solution)/shard_map/ppermute | solution.py:20
  113.2 17.5 %copy-start.13 = (f32[256,512]{1,0:T(8,128)}, f32[256,512]{1,0:T(8,128)S(1)}, u32[]{:S(2)}) copy-start(f32[256,512]{1,0:T(8,128)S(1)} %get-tuple-element.38) | copy-start | bytes 1572868
  116.1 8.6 %copy-start.1 = (f32[512,768]{1,0:T(8,128)S(1)}, f32[512,768]{1,0:T(8,128)}, u32[]{:S(2)}) copy-start(f32[512,768]{1,0:T(8,128)} %get-tuple-element.5) | copy-start | bytes 4718596
  116.1 8.6 %copy-start.2 = (f32[512,768]{1,0:T(8,128)S(1)}, f32[512,768]{1,0:T(8,128)}, u32[]{:S(2)}) copy-start(f32[512,768]{1,0:T(8,128)} %get-tuple-element.6) | copy-start | bytes 4718596
  121.7 9.0 %collective-permute-start.4 = (f32[128,512]{1,0:T(8,128)S(1)}, f32[128,512]{1,0:T(8,128)S(1)}, u32[]{:S(2)}, u32[]{:S(2)}) collective-permute-start(f32[128,512]{1,0:T(8,128)S(1)} %get-tuple-element.23), channel_id=1, source_target_pairs={{0,4},{4,8},{8,12},{1,5},{5,9},{9,13},{2,6},{6,10},{10,14},{3,7},{... | collective-permute-start | bytes 786440 | tf_op jit(solution)/shard_map/ppermute | solution.py:17
  123.0 7.7 %collective-permute-start.5 = (f32[128,512]{1,0:T(8,128)S(1)}, f32[128,512]{1,0:T(8,128)S(1)}, u32[]{:S(2)}, u32[]{:S(2)}) collective-permute-start(f32[128,512]{1,0:T(8,128)S(1)} %get-tuple-element.24), channel_id=1, source_target_pairs={{4,0},{8,4},{12,8},{5,1},{9,5},{13,9},{6,2},{10,6},{14,10},{7,3},{... | collective-permute-start | bytes 786440 | tf_op jit(solution)/shard_map/ppermute | solution.py:20
  131.7 8.5 %collective-permute-start.6 = (f32[512,128]{1,0:T(8,128)}, f32[512,128]{1,0:T(8,128)}, u32[]{:S(2)}, u32[]{:S(2)}) collective-permute-start(f32[512,128]{1,0:T(8,128)} %get-tuple-element.19), channel_id=1, source_target_pairs={{0,1},{1,2},{2,3},{4,5},{5,6},{6,7},{8,9},{9,10},{10,11},{12,13},{... | collective-permute-start | bytes 786440 | tf_op jit(solution)/shard_map/ppermute | solution.py:17
  135.8 9.8 %collective-permute-start.7 = (f32[512,128]{1,0:T(8,128)}, f32[512,128]{1,0:T(8,128)}, u32[]{:S(2)}, u32[]{:S(2)}) collective-permute-start(f32[512,128]{1,0:T(8,128)} %get-tuple-element.20), channel_id=1, source_target_pairs={{1,0},{2,1},{3,2},{5,4},{6,5},{7,6},{9,8},{10,9},{11,10},{13,12},{... | collective-permute-start | bytes 786440 | tf_op jit(solution)/shard_map/ppermute | solution.py:20
  139.7 107.3 %all-reduce.3.cloned.1.call-start = ((), (), s32[]{:S(2)}) async-start(), calls=%async_computation.2 | async-start | bytes 131072 | tf_op jit(solution)/shard_map/psum | solution.py:123
  139.7 16.6 %copy-start.6 = (f32[512,512]{1,0:T(8,128)S(1)}, f32[512,512]{1,0:T(8,128)}, u32[]{:S(2)}) copy-start(f32[512,512]{1,0:T(8,128)} %copy-done.5) | copy-start | bytes 3145732
  139.7 16.6 %copy-start.8 = (f32[512,512]{1,0:T(8,128)S(1)}, f32[512,512]{1,0:T(8,128)}, u32[]{:S(2)}) copy-start(f32[512,512]{1,0:T(8,128)} %copy-done.7) | copy-start | bytes 3145732
  156.3 10.9 %copy-start = (f32[512,768]{1,0:T(8,128)S(1)}, f32[512,768]{1,0:T(8,128)}, u32[]{:S(2)}) copy-start(f32[512,768]{1,0:T(8,128)} %get-tuple-element.8) | copy-start | bytes 4718596
  175.5 36.0 %copy-start.19 = (f32[256,512]{1,0:T(8,128)S(1)}, f32[256,512]{1,0:T(8,128)}, u32[]{:S(2)}) copy-start(f32[256,512]{1,0:T(8,128)} %param.4) | copy-start | bytes 1572868
  (16 other events, 44.6 us)
Sparse Core Ops, SparseCore 0:
  139.8 23.7 reduce-scatter.1
  211.6 35.2 all-reduce.2
where the time goes:
time: 269 us; the launch traced here: 264 us
  matrix products  88.7 us (33%)
  blocking collectives  46.4 us (17%)
  waiting for transfers between devices  46.1 us (17%)
  other arithmetic  44 us (16%)
  between operations  17.6 us (7%)
  starting transfers between devices  17.1 us (6%)
  local copies, waits for them, and re-layouts  4.45 us (2%)
    dot_general x4, matrix products, forward(): lax.dot_general(jnp.concatenate(row_tables, 1), across, (((0,), (0,)), ((...  39.2 us
    psum x1, waiting for transfers between devices, per_device(): owner_grad = lax.psum(owner_grad, 'col')  34.5 us
    psum x1, blocking collectives, per_device(): loss = 0.5 * lax.psum(local_squares, ('row', 'col'))  31.1 us
    dot_general x4, matrix products, forward(): across = jnp.dot(field, jnp.concatenate(col_tables, 1), precision=HIGHEST)  23.9 us
    sin x3, other arithmetic, tables(): return (jnp.cos(phase), jnp.sin(phase))  21.8 us
    dot_general x3, matrix products, inverse(): jnp.dot(jnp.concatenate(row_tables, 0), jnp.concatenate([real_part, imag_...  16.3 us
    ppermute x4, starting transfers between devices, padded(): lax.ppermute(lax.slice_in_dim(block, block.shape[dim] - width, None, axis...  11.3 us
    ppermute x4, waiting for transfers between devices, padded(): lax.ppermute(lax.slice_in_dim(block, 0, width, axis=dim), axis, backward)  9.63 us
  transfers between devices with their start and end apart: 10, of which 5 were waited for; matrix products, arithmetic and copies ran while one was open for 33% of the time, Pallas kernels for 0%

commit v1 on v0

v1 whole, which is shorter than its diff:
```python
import functools
import math

import jax
import jax.numpy as jnp
import numpy as np
from jax import lax
from jax.experimental import pallas as pl
from jax.experimental.pallas import tpu as pltpu
from jax.sharding import PartitionSpec as P

EPSILON = 1e-06
MESH = pl.DeviceIdType.MESH
VMEM = pltpu.VMEM
AROUND = [(a, b) for a in (-1, 0, 1) for b in (-1, 0, 1) if (a, b) != (0, 0)]


def here(row, col, n_row, n_col):
    return (row >= 0) & (row < n_row) & (col >= 0) & (col < n_col)


def greet(row, col, n_row, n_col):
    barrier = pltpu.get_barrier_semaphore()
    count = n_row + n_col - 2
    for s in range(1, n_row):
        pl.semaphore_signal(
            barrier, inc=1, device_id={"row": lax.rem(row + s, n_row)}, device_id_type=MESH
        )
    for s in range(1, n_col):
        pl.semaphore_signal(
            barrier, inc=1, device_id={"col": lax.rem(col + s, n_col)}, device_id_type=MESH
        )
    for dr, dc in AROUND:
        if dc == 0 or dr == 0:
            continue
        there = here(row + dr, col + dc, n_row, n_col)

        @pl.when(there)
        def _():
            pl.semaphore_signal(
                barrier, inc=1, device_id={"row": row + dr, "col": col + dc}, device_id_type=MESH
            )

        count = count + jnp.where(there, 1, 0)
    pl.semaphore_wait(barrier, count)


BF16 = jnp.bfloat16
F32 = jnp.float32


def spans(tile, margin):
    inner = {-1: (0, margin), 0: (0, tile), 1: (tile - margin, margin)}
    outer = {-1: (tile + margin, margin), 0: (0, tile), 1: (tile, margin)}
    return inner, outer


def at(ref, rows, cols):
    return ref.at[pl.ds(*rows), pl.ds(*cols)]


def folded(x):
    rows, cols = x.shape
    if rows % 8:
        x = jnp.concatenate([x, jnp.zeros((8 - rows % 8, cols), F32)], axis=0)
        rows = x.shape[0]
    x = (x * x).reshape(rows // 8, 8, cols).sum(axis=0)
    total = x[:, :128]
    for at_col in range(128, cols, 128):
        total = total + x[:, at_col : at_col + 128]
    return total


def halves(x):
    high = x.astype(BF16)
    return high, (x - high.astype(F32)).astype(BF16)


def dot3(a, b, flip=False):
    dims = (((1,), (1 if flip else 0,)), ((), ()))
    dot = lambda p, q: lax.dot_general(p, q, dims, preferred_element_type=F32)
    return dot(a[0], b[0]) + (dot(a[0], b[1]) + dot(a[1], b[0]))


def body(
    n_row, n_col, observed, estimate, kernel, t_hi, t_lo, f_hi, f_lo, i_hi, i_lo, refined, new_kernel,
    table, fwd_c, fwd_s, inv_c, inv_s, wide, full, xs, ys, spec_i, spec_k, spec_r, grad, kgrad, land,
    rland, cpart, cland, pieces, srow, scol, sums, *sems,
):
    (hs, hr, ks, kr, bs, br, rs, rr, cs, cr, gs, gr, as_, ar, es, er) = sems
    row, col = lax.axis_index("row"), lax.axis_index("col")
    tile_rows, tile_cols = observed.shape
    owner, side = kernel.shape
    margin = side // 2
    cols_long = tile_cols + side
    rows_long = tile_rows + side
    half = cols_long // 2
    scale = 2.0 / (rows_long * cols_long) / side
    in_r, out_r = spans(tile_rows, margin)
    in_c, out_c = spans(tile_cols, margin)

    def copy(src, dst, ssem, rsem, **target):
        return pltpu.make_async_remote_copy(
            src_ref=src, dst_ref=dst, send_sem=ssem, recv_sem=rsem,
            device_id=target, device_id_type=MESH,
        )

    def halo(i):
        dr, dc = AROUND[i]
        return copy(
            at(estimate, in_r[dr], in_c[dc]), at(wide, out_r[-dr], out_c[-dc]),
            hs.at[i], hr.at[i], row=row + dr, col=col + dc,
        )

    def border(i):
        dr, dc = AROUND[i]
        return copy(
            at(grad, out_r[dr], out_c[dc]), at(land, out_r[dr], out_c[dc]),
            bs.at[i], br.at[i], row=row + dr, col=col + dc,
        )

    def target_of(i):
        dr, dc = AROUND[i]
        return here(row + dr, col + dc, n_row, n_col)

    def source_of(i):
        dr, dc = AROUND[i]
        return here(row - dr, col - dc, n_row, n_col)

    def row_peer(s):
        return lax.rem(row + s, n_row)

    def col_peer(s):
        return lax.rem(col + s, n_col)

    def block(r):
        return pl.ds(pl.multiple_of(r * owner, owner), owner)

    greet(row, col, n_row, n_col)
    gathers = [
        copy(kernel, full.at[block(row), :], ks.at[s - 1], kr.at[s - 1], row=row_peer(s))
        for s in range(1, n_row)
    ]
    for one in gathers:
        one.start()
    for i in range(8):

        @pl.when(target_of(i))
        def _():
            halo(i).start()

    for i, (dr, dc) in enumerate(AROUND):

        @pl.when(jnp.logical_not(source_of(i)))
        def _():
            wide[pl.ds(*out_r[-dr]), pl.ds(*out_c[-dc])] = jnp.zeros(
                (out_r[-dr][1], out_c[-dc][1]), F32
            )

    def angles(high, low, a):
        ch, sh = high[0, pl.ds(a, 1), :], high[1, pl.ds(a, 1), :]
        cl, sl = low[0], low[1]
        return ch * cl - sh * sl, sh * cl + ch * sl

    def fill(high, low, put):
        step = low.shape[1]

        def one(a, _):
            put(pl.ds(pl.multiple_of(a * step, step), step), *angles(high, low, a))
            return 0

        lax.fori_loop(0, high.shape[1], one, 0)

    def put_table(rows, c, s):
        for q, v in enumerate((c, -s)):
            for level, part in enumerate(halves(v)):
                table[level, rows, q * half : (q + 1) * half] = part

    def put_pair(c_ref, s_ref):
        def put(rows, c, s):
            for ref, v in ((c_ref, c), (s_ref, s)):
                for level, part in enumerate(halves(v)):
                    ref[level, rows, :] = part

        return put

    fill(t_hi, t_lo, put_table)
    fill(f_hi, f_lo, put_pair(fwd_c, fwd_s))
    fill(i_hi, i_lo, put_pair(inv_c, inv_s))

    def pair(ref, rows, cols=slice(None)):
        return ref[0, rows, cols], ref[1, rows, cols]

    def store(ref, rows, x):
        high, low = halves(x)
        ref[0, rows, :] = high
        ref[1, rows, :] = low

    lag, own_cols = slice(0, side), slice(margin, margin + tile_cols)
    beside = slice(margin + tile_cols, margin + tile_cols + side)
    all_cols = slice(margin, margin + tile_cols + side)
    near, far = slice(0, tile_rows), slice(tile_rows, rows_long)

    def rows_forward(spec, freqs, x):
        p, q = dot3(pair(fwd_c, freqs), x), dot3(pair(fwd_s, freqs), x)
        spec[freqs, :half] = p[:, :half] + q[:, half:]
        spec[freqs, half:] = p[:, half:] - q[:, :half]

    def rows_inverse(freqs, x):
        p, q = dot3(pair(inv_c, slice(None), freqs), x), dot3(pair(inv_s, slice(None), freqs), x)
        return jnp.concatenate([p[:, :half] - q[:, half:], p[:, half:] + q[:, :half]], axis=1)

    def multiply(dst, a, b, conj):
        def one(k, _):
            rows = pl.ds(pl.multiple_of(k * 32, 32), 32)
            ar_, ai_, br_, bi_ = a[rows, :half], a[rows, half:], b[rows, :half], b[rows, half:]
            if conj:
                re, im = ar_ * br_ + ai_ * bi_, ai_ * br_ - ar_ * bi_
            else:
                re, im = ar_ * br_ - ai_ * bi_, ar_ * bi_ + ai_ * br_
            for q, v in enumerate((re, im)):
                for level, part in enumerate(halves(v)):
                    dst[level, rows, q * half : (q + 1) * half] = part
            return 0

        lax.fori_loop(0, rows_long // 32, one, 0)

    grad[near, :] = dot3(halves(estimate[...]), pair(table, own_cols))

    full[block(row), :] = kernel[...]
    for one in gathers:
        one.wait()
    store(ys, near, dot3(halves(full[...]), pair(table, lag)))
    for freqs in (near, far):
        rows_forward(spec_k, freqs, pair(ys, near))

    for i in range(8):

        @pl.when(source_of(i))
        def _():
            halo(i).wait_recv()

    own = grad[near, :] + dot3(halves(wide[near, tile_cols:]), pair(table, beside))
    other = dot3(halves(wide[far, :]), pair(table, all_cols))
    store(xs, near, own + other)
    store(xs, far, own - other)
    rows_forward(spec_i, near, pair(xs, near))
    rows_forward(spec_i, far, pair(xs, far))
    multiply(xs, spec_i, spec_k, False)
    mixed = rows_inverse(slice(None), pair(xs, slice(None)))
    resid = dot3(halves(mixed), pair(table, own_cols), True) * scale - observed[...]
    sums[0] = folded(resid)
    store(ys, near, dot3(halves(resid), pair(table, own_cols)))
    for freqs in (near, far):
        rows_forward(spec_r, freqs, pair(ys, near))

    multiply(xs, spec_r, spec_i, True)
    mixed = rows_inverse(slice(None), pair(xs, slice(None)))
    kgrad[...] = dot3(halves(mixed), pair(table, lag), True) * scale
    parts = [
        copy(kgrad.at[block(row_peer(s)), :], rland.at[s - 1], rs.at[s - 1], rr.at[s - 1], row=row_peer(s))
        for s in range(1, n_row)
    ]
    for one in parts:
        one.start()

    multiply(xs, spec_r, spec_k, True)
    even = rows_inverse(near, pair(xs, near))
    odd = rows_inverse(far, pair(xs, far))
    store(ys, far, even - odd)
    store(ys, near, even + odd)
    grad[far, :] = dot3(pair(ys, far), pair(table, all_cols), True) * scale
    for i in range(8):
        if AROUND[i][0] != 0:

            @pl.when(target_of(i))
            def _():
                border(i).start()

    grad[near, tile_cols:] = dot3(pair(ys, near), pair(table, beside), True) * scale
    for i in range(8):
        if AROUND[i][0] == 0:

            @pl.when(target_of(i))
            def _():
                border(i).start()

    mine = kgrad[block(row), :]
    for s, one in enumerate(parts):
        one.wait()
        mine = mine + rland[s]
    few = owner // n_col
    for c in range(n_col):
        cpart[c] = mine[c * few : (c + 1) * few]
    parts = [
        copy(cpart.at[col_peer(s)], cland.at[s - 1], cs.at[s - 1], cr.at[s - 1], col=col_peer(s))
        for s in range(1, n_col)
    ]
    for one in parts:
        one.start()
    refined[...] = dot3(pair(ys, near), pair(table, own_cols), True) * scale
    piece = cpart[col]
    for s, one in enumerate(parts):
        one.wait()
        piece = piece + cland[s]
    pieces[col] = piece
    gathers = [
        copy(pieces.at[col], pieces.at[col], gs.at[s - 1], gr.at[s - 1], col=col_peer(s))
        for s in range(1, n_col)
    ]
    for one in gathers:
        one.start()
    sums[2] = folded(piece)
    for i, (dr, dc) in enumerate(AROUND):

        @pl.when(source_of(i))
        def _():
            border(i).wait_recv()
            region = (pl.ds(*in_r[-dr]), pl.ds(*in_c[-dc]))
            refined[region] = refined[region] + land[pl.ds(*out_r[dr]), pl.ds(*out_c[dc])]

    sums[1] = folded(refined[...])
    srow[row] = sums[...]
    parts = [
        copy(srow.at[row], srow.at[row], as_.at[s - 1], ar.at[s - 1], row=row_peer(s))
        for s in range(1, n_row)
    ]
    for one in parts:
        one.start()
    for one in parts:
        one.wait()
    added = srow[0]
    for r in range(1, n_row):
        added = added + srow[r]
    scol[col] = added
    parts = [
        copy(scol.at[col], scol.at[col], es.at[s - 1], er.at[s - 1], col=col_peer(s))
        for s in range(1, n_col)
    ]
    for one in parts:
        one.start()
    for one in gathers:
        one.wait()
    for one in parts:
        one.wait()
    added = scol[0]
    for c in range(1, n_col):
        added = added + scol[c]
    loss = 0.5 * jnp.sum(added[0], keepdims=True)
    image_norm = jnp.sum(added[1], keepdims=True)
    kernel_norm = jnp.sum(added[2], keepdims=True)
    refined[...] = estimate[...] - refined[...] * (loss / (image_norm + EPSILON))
    rate = 0.25 * loss / (kernel_norm + EPSILON)
    for c in range(n_col):
        rows = slice(c * few, (c + 1) * few)
        new_kernel[rows, :] = kernel[rows, :] - pieces[c] * rate
    for i in range(8):

        @pl.when(target_of(i))
        def _():
            halo(i).wait_send()
            border(i).wait_send()


def turns(places, freqs, period, step):
    def both(some, others):
        phase = np.mod(np.outer(some, others), period) * (2 * math.pi / period)
        return jnp.asarray(np.stack([np.cos(phase), np.sin(phase)]).astype(np.float32))

    return both(places[::step], freqs), both(places[:step] - places[0], freqs)


def per_device(n_row, n_col, observed, estimate, kernel):
    tile_rows, tile_cols = observed.shape
    owner, side = kernel.shape
    margin = side // 2
    rows_long, cols_long = tile_rows + side, tile_cols + side
    half = cols_long // 2
    places = np.concatenate([np.arange(cols_long) - margin, np.arange(margin) - margin])
    t_hi, t_lo = turns(places, 2 * np.arange(half) + 1, 2 * cols_long, 16)
    freqs = np.concatenate([np.arange(0, rows_long, 2), np.arange(1, rows_long, 2)])
    centred = np.arange(side) - margin
    i_hi, i_lo = turns(centred, freqs, rows_long, 16)
    f_hi, f_lo = turns(freqs, centred, rows_long, 16)
    dma = pltpu.SemaphoreType.DMA
    more_r, more_c = max(n_row - 1, 1), max(n_col - 1, 1)
    few = owner // n_col
    spectrum = VMEM((rows_long, cols_long), F32)
    split = VMEM((2, rows_long, cols_long), BF16)
    return pl.pallas_call(
        functools.partial(body, n_row, n_col),
        out_shape=(
            jax.ShapeDtypeStruct((tile_rows, tile_cols), F32),
            jax.ShapeDtypeStruct((owner, side), F32),
        ),
        in_specs=[pl.BlockSpec(memory_space=VMEM)] * 9,
        out_specs=(pl.BlockSpec(memory_space=VMEM),) * 2,
        scratch_shapes=[
            VMEM((2, len(places), cols_long), BF16),
            VMEM((2, rows_long, side), BF16),
            VMEM((2, rows_long, side), BF16),
            VMEM((2, side, rows_long), BF16),
            VMEM((2, side, rows_long), BF16),
            spectrum,
            VMEM((side, side), F32),
            split,
            split,
            spectrum,
            spectrum,
            spectrum,
            spectrum,
            VMEM((side, side), F32),
            spectrum,
            VMEM((more_r, owner, side), F32),
            VMEM((n_col, few, side), F32),
            VMEM((more_c, few, side), F32),
            VMEM((n_col, few, side), F32),
            VMEM((n_row, 3, 8, 128), F32),
            VMEM((n_col, 3, 8, 128), F32),
            VMEM((3, 8, 128), F32),
            dma((8,)), dma((8,)),
            dma((more_r,)), dma((more_r,)),
            dma((8,)), dma((8,)),
            dma((more_r,)), dma((more_r,)),
            dma((more_c,)), dma((more_c,)),
            dma((more_c,)), dma((more_c,)),
            dma((more_r,)), dma((more_r,)),
            dma((more_c,)), dma((more_c,)),
        ],
        compiler_params=pltpu.CompilerParams(
            collective_id=0, has_side_effects=True, vmem_limit_bytes=56 * 1024 * 1024
        ),
        name="deconvolve",
    )(observed, estimate, kernel, t_hi, t_lo, f_hi, f_lo, i_hi, i_lo)


def solution(mesh):
    placed = (P(("groups", "row"), "col"), P(("groups", "row"), "col"), P(("groups", "row"), None))
    return jax.shard_map(
        functools.partial(per_device, mesh.shape["row"], mesh.shape["col"]),
        mesh=mesh,
        in_specs=placed,
        out_specs=(P(("groups", "row"), "col"), P(("groups", "row"), None)),
        check_vma=False,
    )
```

time: 269 us -> 49 us (0.18); the launches traced: 264 us -> 48.9 us
  matrix products: 88.7 us -> 0 us
  blocking collectives: 46.4 us -> 0 us
  waiting for transfers between devices: 46.1 us -> 0 us
  Pallas kernels: 0 us -> 45.7 us
  other arithmetic: 44 us -> 0 us
  starting transfers between devices: 17.1 us -> 0 us
  between operations: 17.6 us -> 0.65 us
    dot_general x14 -> x0, matrix products: 88.7 us -> none  [the longest x4 39.2 us: forward(): lax.dot_general(jnp.concatenate(row_tables, 1), across, (((0,), (0,)), ((...]
    pallas_call x0 -> x1, Pallas kernels: none -> 45.7 us  [per_device(): pl.pallas_call(functools.partial(body, n_row, n_col), out_shape=(jax.Shap...]
    psum x2 -> x0, blocking collectives: 37.3 us -> none  [the longest x1 31.1 us: per_device(): loss = 0.5 * lax.psum(local_squares, ('row', 'col'))]
    psum x1 -> x0, waiting for transfers between devices: 34.5 us -> none  [per_device(): owner_grad = lax.psum(owner_grad, 'col')]
    sin x3 -> x0, other arithmetic: 21.8 us -> none  [tables(): return (jnp.cos(phase), jnp.sin(phase))]
    ppermute x8 -> x0, starting transfers between devices: 17 us -> none  [the longest x4 11.3 us: padded(): lax.ppermute(lax.slice_in_dim(block, block.shape[dim] - width, None, axis...]
    ppermute x8 -> x0, waiting for transfers between devices: 11.5 us -> none  [the longest x4 9.63 us: padded(): lax.ppermute(lax.slice_in_dim(block, 0, width, axis=dim), axis, backward)]
    all_gather x1 -> x0, blocking collectives: 9.12 us -> none  [collect(): return lax.all_gather(kernel, 'row', axis=0, tiled=True)]
  transfers between devices with their start and end apart: 10 -> 0, of which waited for: 5 -> 0; matrix products, arithmetic and copies ran while one was open for 33% -> 0% of each run, Pallas kernels for 0% -> 0%
where the time goes in v1:
time: 49 us; the launch traced here: 48.9 us
  Pallas kernels  45.7 us (93%)
  local copies, waits for them, and re-layouts  2.53 us (5%)
  between operations  0.65 us (1%)
    pallas_call x1, Pallas kernels, per_device(): pl.pallas_call(functools.partial(body, n_row, n_col), out_shape=(jax.Shap...  45.7 us
    unnamed x4, local copies, waits for them, and re-layouts  2.53 us

profile of v1, /device:TPU:0, one launch (start us, length us, event | category | flops | bytes accessed | tf_op | source)
XLA Modules:
  0.0 48.9 jit_solution(2092846124510170623)
XLA Ops:
  0.6 45.7 %deconvolve.1 = (f32[256,512]{1,0:T(8,128)}, f32[64,256]{1,0:T(8,128)}) custom-call(f32[256,512]{1,0:T(8,128)} %observed.1, f32[256,512]{1,0:T(8,128)} %estimate.1, f32[64,256]{1,0:T(8,128)} %kernel.1, f32[2,56,384]{2,1,0:T(8,128)} %constant.12.clone.t_hi, f32[2,16,384]{2,1,0:T(8,128)} %constant.13.clone.t_lo, f32[2,32,256]{2,1,0:T(8,128)} %constant.16.clone.f_hi, ...), custom_call_target="tpu_custom_call" | custom-call | tf_op jit(solution)/shard_map/deconvolve/pallas_call | solution.py:390
  46.3 0.0 copy-start
  46.3 1.9 %copy.13 = f32[256,512]{1,0:T(8,128)} copy(f32[256,512]{1,0:T(8,128)} %get-tuple-element.4) | data formatting | bytes 1048576
  48.2 0.0 copy-done
  48.2 0.6 %copy.14 = f32[64,256]{1,0:T(8,128)} copy(f32[64,256]{1,0:T(8,128)S(1)} %copy-done) | data formatting | bytes 131072
Async XLA Ops:
  46.3 1.9 %copy-start = (f32[64,256]{1,0:T(8,128)S(1)}, f32[64,256]{1,0:T(8,128)}, u32[]{:S(2)}) copy-start(f32[64,256]{1,0:T(8,128)} %get-tuple-element.5) | copy-start | bytes 196612

commit v2 on v1

--- a/solution.py
+++ b/solution.py
@@ -11,6 +11,7 @@
 
 EPSILON = 1e-06
 MESH = pl.DeviceIdType.MESH
+FEW = 16
 VMEM = pltpu.VMEM
 AROUND = [(a, b) for a in (-1, 0, 1) for b in (-1, 0, 1) if (a, b) != (0, 0)]
 
@@ -19,8 +20,23 @@
     return (row >= 0) & (row < n_row) & (col >= 0) & (col < n_col)
 
 
+def others(n_row, n_col):
+    return [(s, t) for s in range(n_row) for t in range(n_col) if (s, t) != (0, 0)]
+
+
+def peer(row, col, s, t, n_row, n_col):
+    return {"row": lax.rem(row + s, n_row), "col": lax.rem(col + t, n_col)}
+
+
 def greet(row, col, n_row, n_col):
     barrier = pltpu.get_barrier_semaphore()
+    if n_row * n_col <= FEW:
+        for s, t in others(n_row, n_col):
+            pl.semaphore_signal(
+                barrier, inc=1, device_id=peer(row, col, s, t, n_row, n_col), device_id_type=MESH
+            )
+        pl.semaphore_wait(barrier, n_row * n_col - 1)
+        return
     count = n_row + n_col - 2
     for s in range(1, n_row):
         pl.semaphore_signal(
@@ -69,6 +85,10 @@
     for at_col in range(128, cols, 128):
         total = total + x[:, at_col : at_col + 128]
     return total
+
+
+def line(x):
+    return jnp.sum(folded(x), axis=0, keepdims=True)
 
 
 def halves(x):
@@ -212,7 +232,7 @@
 
     def multiply(dst, a, b, conj):
         def one(k, _):
-            rows = pl.ds(pl.multiple_of(k * 32, 32), 32)
+            rows = pl.ds(k * 32, 32)
             ar_, ai_, br_, bi_ = a[rows, :half], a[rows, half:], b[rows, :half], b[rows, half:]
             if conj:
                 re, im = ar_ * br_ + ai_ * bi_, ai_ * br_ - ar_ * bi_
@@ -223,7 +243,8 @@
                     dst[level, rows, q * half : (q + 1) * half] = part
             return 0
 
-        lax.fori_loop(0, rows_long // 32, one, 0)
+        for k in range(rows_long // 32):
+            one(k, 0)
 
     grad[near, :] = dot3(halves(estimate[...]), pair(table, own_cols))
 
@@ -249,7 +270,8 @@
     multiply(xs, spec_i, spec_k, False)
     mixed = rows_inverse(slice(None), pair(xs, slice(None)))
     resid = dot3(halves(mixed), pair(table, own_cols), True) * scale - observed[...]
-    sums[0] = folded(resid)
+    sums[...] = jnp.zeros_like(sums)
+    sums[0:1] = line(resid)
     store(ys, near, dot3(halves(resid), pair(table, own_cols)))
     for freqs in (near, far):
         rows_forward(spec_r, freqs, pair(ys, near))
@@ -299,56 +321,70 @@
     for one in parts:
         one.start()
     refined[...] = dot3(pair(ys, near), pair(table, own_cols), True) * scale
+    for i, (dr, dc) in enumerate(AROUND):
+
+        @pl.when(source_of(i))
+        def _():
+            border(i).wait_recv()
+            region = (pl.ds(*in_r[-dr]), pl.ds(*in_c[-dc]))
+            refined[region] = refined[region] + land[pl.ds(*out_r[dr]), pl.ds(*out_c[dc])]
+
+    sums[1:2] = line(refined[...])
     piece = cpart[col]
     for s, one in enumerate(parts):
         one.wait()
         piece = piece + cland[s]
     pieces[col] = piece
+    sums[2:3] = line(piece)
+
     gathers = [
         copy(pieces.at[col], pieces.at[col], gs.at[s - 1], gr.at[s - 1], col=col_peer(s))
         for s in range(1, n_col)
     ]
-    for one in gathers:
-        one.start()
-    sums[2] = folded(piece)
-    for i, (dr, dc) in enumerate(AROUND):
-
-        @pl.when(source_of(i))
-        def _():
-            border(i).wait_recv()
-            region = (pl.ds(*in_r[-dr]), pl.ds(*in_c[-dc]))
-            refined[region] = refined[region] + land[pl.ds(*out_r[dr]), pl.ds(*out_c[dc])]
-
-    sums[1] = folded(refined[...])
-    srow[row] = sums[...]
-    parts = [
-        copy(srow.at[row], srow.at[row], as_.at[s - 1], ar.at[s - 1], row=row_peer(s))
-        for s in range(1, n_row)
-    ]
-    for one in parts:
-        one.start()
-    for one in parts:
-        one.wait()
-    added = srow[0]
-    for r in range(1, n_row):
-        added = added + srow[r]
-    scol[col] = added
-    parts = [
-        copy(scol.at[col], scol.at[col], es.at[s - 1], er.at[s - 1], col=col_peer(s))
-        for s in range(1, n_col)
-    ]
-    for one in parts:
-        one.start()
+
+    def total_of(buf):
+        added = buf[0]
+        for k in range(1, buf.shape[0]):
+            added = added + buf[k]
+        return added
+
+    if n_row * n_col <= FEW:
+        me = row * n_col + col
+        srow[me] = sums[...]
+        parts = [
+            copy(srow.at[me], srow.at[me], as_.at[k], ar.at[k], **peer(row, col, s, t, n_row, n_col))
+            for k, (s, t) in enumerate(others(n_row, n_col))
+        ]
+        for one in parts + gathers:
+            one.start()
+        for one in parts:
+            one.wait()
+        added = total_of(srow)
+    else:
+        srow[row] = sums[...]
+        parts = [
+            copy(srow.at[row], srow.at[row], as_.at[s - 1], ar.at[s - 1], row=row_peer(s))
+            for s in range(1, n_row)
+        ]
+        for one in parts + gathers:
+            one.start()
+        for one in parts:
+            one.wait()
+        scol[col] = total_of(srow)
+        parts = [
+            copy(scol.at[col], scol.at[col], es.at[s - 1], er.at[s - 1], col=col_peer(s))
+            for s in range(1, n_col)
+        ]
+        for one in parts:
+            one.start()
+        for one in parts:
+            one.wait()
+        added = total_of(scol)
     for one in gathers:
         one.wait()
-    for one in parts:
-        one.wait()
-    added = scol[0]
-    for c in range(1, n_col):
-        added = added + scol[c]
-    loss = 0.5 * jnp.sum(added[0], keepdims=True)
-    image_norm = jnp.sum(added[1], keepdims=True)
-    kernel_norm = jnp.sum(added[2], keepdims=True)
+    loss = 0.5 * jnp.sum(added[0:1], keepdims=True)
+    image_norm = jnp.sum(added[1:2], keepdims=True)
+    kernel_norm = jnp.sum(added[2:3], keepdims=True)
     refined[...] = estimate[...] - refined[...] * (loss / (image_norm + EPSILON))
     rate = 0.25 * loss / (kernel_norm + EPSILON)
     for c in range(n_col):
@@ -385,6 +421,7 @@
     dma = pltpu.SemaphoreType.DMA
     more_r, more_c = max(n_row - 1, 1), max(n_col - 1, 1)
     few = owner // n_col
+    firsts = n_row * n_col if n_row * n_col <= FEW else n_row
     spectrum = VMEM((rows_long, cols_long), F32)
     split = VMEM((2, rows_long, cols_long), BF16)
     return pl.pallas_call(
@@ -415,16 +452,16 @@
             VMEM((n_col, few, side), F32),
             VMEM((more_c, few, side), F32),
             VMEM((n_col, few, side), F32),
-            VMEM((n_row, 3, 8, 128), F32),
-            VMEM((n_col, 3, 8, 128), F32),
-            VMEM((3, 8, 128), F32),
+            VMEM((firsts, 8, 128), F32),
+            VMEM((n_col, 8, 128), F32),
+            VMEM((8, 128), F32),
             dma((8,)), dma((8,)),
             dma((more_r,)), dma((more_r,)),
             dma((8,)), dma((8,)),
             dma((more_r,)), dma((more_r,)),
             dma((more_c,)), dma((more_c,)),
             dma((more_c,)), dma((more_c,)),
-            dma((more_r,)), dma((more_r,)),
+            dma((firsts,)), dma((firsts,)),
             dma((more_c,)), dma((more_c,)),
         ],
         compiler_params=pltpu.CompilerParams(

time: 49 us -> 46.4 us (0.947)
  Pallas kernels: 45.7 us -> 43.1 us
    pallas_call x1, Pallas kernels: 45.7 us -> 43.1 us  [per_device(): pl.pallas_call(functools.partial(body, n_row, n_col), out_shape=(jax.Shap...]
where the time goes in v2:
time: 46.4 us; the launch traced here: 46.3 us
  Pallas kernels  43.1 us (93%)
  local copies, waits for them, and re-layouts  2.53 us (5%)
  between operations  0.65 us (1%)
    pallas_call x1, Pallas kernels, per_device(): pl.pallas_call(functools.partial(body, n_row, n_col), out_shape=(jax.Shap...  43.1 us
    unnamed x4, local copies, waits for them, and re-layouts  2.53 us

profile of v2, /device:TPU:0, one launch (start us, length us, event | category | flops | bytes accessed | tf_op | source)
XLA Modules:
  0.0 46.3 jit_solution(5674135980345642303)
XLA Ops:
  0.6 43.1 %deconvolve.1 = (f32[256,512]{1,0:T(8,128)}, f32[64,256]{1,0:T(8,128)}) custom-call(f32[256,512]{1,0:T(8,128)} %observed.1, f32[256,512]{1,0:T(8,128)} %estimate.1, f32[64,256]{1,0:T(8,128)} %kernel.1, f32[2,56,384]{2,1,0:T(8,128)} %constant.12.clone.t_hi, f32[2,16,384]{2,1,0:T(8,128)} %constant.13.clone.t_lo, f32[2,32,256]{2,1,0:T(8,128)} %constant.16.clone.f_hi, ...), custom_call_target="tpu_custom_call" | custom-call | tf_op jit(solution)/shard_map/deconvolve/pallas_call | solution.py:427
  43.7 0.0 copy-start
  43.7 1.9 %copy.13 = f32[256,512]{1,0:T(8,128)} copy(f32[256,512]{1,0:T(8,128)} %get-tuple-element.4) | data formatting | bytes 1048576
  45.6 0.0 copy-done
  45.6 0.6 %copy.14 = f32[64,256]{1,0:T(8,128)} copy(f32[64,256]{1,0:T(8,128)S(1)} %copy-done) | data formatting | bytes 131072
Async XLA Ops:
  43.7 1.9 %copy-start = (f32[64,256]{1,0:T(8,128)S(1)}, f32[64,256]{1,0:T(8,128)}, u32[]{:S(2)}) copy-start(f32[64,256]{1,0:T(8,128)} %get-tuple-element.5) | copy-start | bytes 196612
